TPU v7x, 32 devices: a whole 2x2x4 slice. The times are simulated.
32 devices in a mesh: gx: 2 (over core), gy: 4 (over z), gz: 4 (over y, x).
Axes of the slice: x: 2, y: 2, z: 4, core: 2. Of those that a mesh axis runs over, the one named last changes fastest.
Arguments:
- density_volume: float32 [64, 512, 512], P('gz', 'gy', 'gx'), may hold values from -4 to 4
Outputs:
- colour: float32 [3, 512, 512], P(None, ('gy', 'gz'), 'gx')
- depth_map: float32 [512, 512], P(('gy', 'gz'), 'gx')
- transparency: float32 [512, 512], P(('gy', 'gz'), 'gx')
All inputs are finite; a program needn't handle non-finite values.
Results may differ from a plain program's by a relative error of at most 0.0003.
Values sent between devices are 32-bit elements; how exact they have to be, the bound alone decides.
No kernel may reach another device: no remote copies, remote signals or barrier semaphores. Data moves between devices by JAX's collectives and lax.ppermute only.
A program may use at most 128 MiB of HBM per device.

v0:
```python
import jax
import jax.numpy as jnp
from jax import lax
from jax.sharding import PartitionSpec as P


def with_halo(shard, sides, width):
    for axis, dim in sides:
        peers, length = (lax.axis_size(axis), shard.shape[dim])
        up = [(i, (i + 1) % peers) for i in range(peers - 1)]
        down = [(j, i) for i, j in up]
        last = lax.slice_in_dim(shard, length - width, length, axis=dim)
        initial = lax.slice_in_dim(shard, 0, width, axis=dim)
        before = lax.ppermute(last, axis, up)
        after = lax.ppermute(initial, axis, down)
        shard = jnp.concatenate([before, shard, after], axis=dim)
    return shard


def fourth(far_low, near_low, near_high, far_high):
    return (far_low - 8.0 * near_low + 8.0 * near_high - far_high) / 12.0


def shade(sample, grad_z, grad_y, grad_x):
    square = grad_z * grad_z + grad_y * grad_y + grad_x * grad_x
    facing = (0.64 * grad_z + 0.6 * grad_y + 0.48 * grad_x) * lax.rsqrt(square + 1.0)
    diffuse = 0.3 + 0.7 * jnp.maximum(facing, 0.0)
    edge_gain = 1.0 + square / (square + 1.0)
    density = jax.nn.softplus(sample) * edge_gain
    colour_red = jax.nn.sigmoid(2.0 * sample) * diffuse
    colour_green = jnp.exp(-0.5 * sample * sample) * diffuse
    colour_blue = jax.nn.sigmoid(-2.0 * sample) * diffuse
    return (density, colour_red, colour_green, colour_blue)


def blend_depth(received):
    through = received[4]
    running = jnp.cumprod(through, axis=0)
    front_pass = jnp.concatenate([jnp.ones_like(running[:1]), running[:-1]], axis=0)
    shaded = jnp.sum(front_pass[None] * received[:4], axis=1)
    return jnp.concatenate([shaded, running[-1:]], axis=0)


def on_device(density_volume):
    cells_z, cells_y, cells_x = density_volume.shape
    depth_count = lax.axis_size("gz")
    depth_index = lax.axis_index("gz")
    total_z = cells_z * depth_count
    depth_step = 2.0 / total_z
    padded = with_halo(density_volume, (("gx", 2), ("gy", 1), ("gz", 0)), 2)
    centre = padded[2:-2, 2:-2, 2:-2]
    grad_z = fourth(
        padded[0:-4, 2:-2, 2:-2],
        padded[1:-3, 2:-2, 2:-2],
        padded[3:-1, 2:-2, 2:-2],
        padded[4:, 2:-2, 2:-2],
    )
    grad_y = fourth(
        padded[2:-2, 0:-4, 2:-2],
        padded[2:-2, 1:-3, 2:-2],
        padded[2:-2, 3:-1, 2:-2],
        padded[2:-2, 4:, 2:-2],
    )
    grad_x = fourth(
        padded[2:-2, 2:-2, 0:-4],
        padded[2:-2, 2:-2, 1:-3],
        padded[2:-2, 2:-2, 3:-1],
        padded[2:-2, 2:-2, 4:],
    )
    density, colour_red, colour_green, colour_blue = shade(centre, grad_z, grad_y, grad_x)
    pixels = cells_y * cells_x
    optical = (density * depth_step).reshape(cells_z, pixels)
    row_iota = lax.broadcasted_iota(jnp.int32, (cells_z, cells_z), 0)
    col_iota = lax.broadcasted_iota(jnp.int32, (cells_z, cells_z), 1)
    lower_tri = (row_iota >= col_iota).astype(jnp.float32)
    inclusive = jnp.dot(
        lower_tri, optical, precision=lax.Precision.HIGHEST, preferred_element_type=jnp.float32
    )
    weight = jnp.exp(-(inclusive - optical)) * (1.0 - jnp.exp(-optical))
    depth_pos = (
        (depth_index * cells_z + jnp.arange(cells_z, dtype=jnp.int32)).astype(jnp.float32) + 0.5
    ) / total_z
    partial_value = jnp.stack(
        [
            jnp.sum(weight * colour_red.reshape(cells_z, pixels), axis=0),
            jnp.sum(weight * colour_green.reshape(cells_z, pixels), axis=0),
            jnp.sum(weight * colour_blue.reshape(cells_z, pixels), axis=0),
            jnp.sum(weight * depth_pos[:, None], axis=0),
            jnp.exp(-inclusive[-1]),
        ]
    ).reshape(5, cells_y, cells_x)
    piece_rows = cells_y // depth_count
    stacked = partial_value.reshape(5, depth_count, piece_rows, cells_x)
    final_image = blend_depth(
        lax.all_to_all(stacked, "gz", split_axis=1, concat_axis=1, tiled=True)
    )
    return (final_image[:3], final_image[3], final_image[4])


def solution(mesh):
    return jax.shard_map(
        on_device,
        mesh=mesh,
        in_specs=(P("gz", "gy", "gx"),),
        out_specs=(P(None, ("gy", "gz"), "gx"), P(("gy", "gz"), "gx"), P(("gy", "gz"), "gx")),
        check_vma=False,
    )
```

profile of v0, /device:TPU:0, one launch (start us, length us, event | category | flops | bytes accessed | tf_op | source)
XLA Modules:
  0.0 101.9 jit_solution(17254441752755021613)
XLA Ops:
  0.6 2.9 %fusion.27 = (f32[16,128,2]{2,1,0:T(8,128)}, f32[16,128,2]{2,1,0:T(8,128)S(1)}) fusion(f32[16,128,256]{2,1,0:T(8,128)} %param.1), kind=kLoop, calls=%fused_computation.73 | loop fusion | bytes 65536 | tf_op jit(solution)/shard_map/slice | solution.py:12
  3.5 0.0 copy-start
  3.5 1.7 %copy.11 = f32[16,128,2]{1,0,2:T(8,128)S(1)} copy(f32[16,128,2]{2,1,0:T(8,128)} %get-tuple-element.23) | data formatting | bytes 32768
  5.2 2.4 %collective-permute-start = (f32[16,128,2]{1,0,2:T(8,128)S(1)}, f32[16,128,2]{1,0,2:T(8,128)S(1)}, u32[]{:S(2)}, u32[]{:S(2)}) collective-permute-start(f32[16,128,2]{1,0,2:T(8,128)S(1)} %copy.11), channel_id=1, source_target_pairs={{0,16},{1,17},{2,18},{3,19},{4,20},{5,21},{6,22},{7,23},{8,24},{9,... | collective-permute-start | bytes 49160 | tf_op jit(solution)/shard_map/ppermute | solution.py:14
  7.6 0.3 copy.12
  7.9 1.3 %collective-permute-start.1 = (f32[16,128,2]{1,0,2:T(8,128)S(1)}, f32[16,128,2]{1,0,2:T(8,128)S(1)}, u32[]{:S(2)}, u32[]{:S(2)}) collective-permute-start(f32[16,128,2]{1,0,2:T(8,128)S(1)} %copy.12), channel_id=1, source_target_pairs={{16,0},{17,1},{18,2},{19,3},{20,4},{21,5},{22,6},{23,7},{24,8},{25... | collective-permute-start | bytes 49160 | tf_op jit(solution)/shard_map/ppermute | solution.py:15
  9.2 0.0 collective-permute-done
  9.2 0.4 copy.6
  9.6 1.4 %collective-permute-done.1 = f32[16,128,2]{1,0,2:T(8,128)S(1)} collective-permute-done((f32[16,128,2]{1,0,2:T(8,128)S(1)}, f32[16,128,2]{1,0,2:T(8,128)S(1)}, u32[]{:S(2)}, u32[]{:S(2)}) %collective-permute-start.1) | collective-permute-done | bytes 16416 | tf_op jit(solution)/shard_map/ppermute | solution.py:15
  11.0 1.4 %copy.7 = f32[16,128,2]{2,1,0:T(8,128)} copy(f32[16,128,2]{1,0,2:T(8,128)S(1)} %collective-permute-done.1) | data formatting | bytes 32768 | tf_op jit(solution)/shard_map/ppermute | solution.py:15
  12.4 0.0 copy-done
  12.5 0.0 copy-start.1
  12.5 1.2 %pad_maximum_fusion.11 = (f32[16,2,260]{2,1,0:T(2,128)S(1)}, f32[16,2,260]{2,1,0:T(2,128)S(1)}) fusion(f32[16,128,2]{2,1,0:T(8,128)} %copy.7, f32[16,128,256]{2,1,0:T(8,128)S(1)} %copy-done, f32[16,128,2]{2,1,0:T(8,128)S(1)} %copy.6), kind=kLoop, calls=%fused_computation.63 | loop fusion | flops 33280 | bytes 2196480 | tf_op jit(solution)/shard_map/slice | solution.py:12
  13.6 4.3 %collective-permute-start.2 = (f32[16,2,260]{2,1,0:T(2,128)S(1)}, f32[16,2,260]{2,1,0:T(2,128)S(1)}, u32[]{:S(2)}, u32[]{:S(2)}) collective-permute-start(f32[16,2,260]{2,1,0:T(2,128)S(1)} %get-tuple-element.20), channel_id=1, source_target_pairs={{0,4},{4,8},{8,12},{1,5},{5,9},{9,13},{2,6},{6,10},{10,14},{3,7},{... | collective-permute-start | bytes 99848 | tf_op jit(solution)/shard_map/ppermute | solution.py:14
  17.9 1.3 %collective-permute-start.3 = (f32[16,2,260]{2,1,0:T(2,128)S(1)}, f32[16,2,260]{2,1,0:T(2,128)S(1)}, u32[]{:S(2)}, u32[]{:S(2)}) collective-permute-start(f32[16,2,260]{2,1,0:T(2,128)S(1)} %get-tuple-element.21), channel_id=1, source_target_pairs={{4,0},{8,4},{12,8},{5,1},{9,5},{13,9},{6,2},{10,6},{14,10},{7,3},{... | collective-permute-start | bytes 99848 | tf_op jit(solution)/shard_map/ppermute | solution.py:15
  19.3 0.4 collective-permute-done.2
  19.7 4.3 %collective-permute-done.3 = f32[16,2,260]{2,1,0:T(2,128)S(1)} collective-permute-done((f32[16,2,260]{2,1,0:T(2,128)S(1)}, f32[16,2,260]{2,1,0:T(2,128)S(1)}, u32[]{:S(2)}, u32[]{:S(2)}) %collective-permute-start.3) | collective-permute-done | bytes 33312 | tf_op jit(solution)/shard_map/ppermute | solution.py:15
  23.9 0.0 copy-done.1
  23.9 0.4 pad_maximum_fusion.8
  24.3 3.4 %collective-permute-start.4 = (f32[2,132,260]{2,1,0:T(8,128)S(1)}, f32[2,132,260]{2,1,0:T(8,128)S(1)}, u32[]{:S(2)}, u32[]{:S(2)}) collective-permute-start(f32[2,132,260]{2,1,0:T(8,128)S(1)} %get-tuple-element.14), channel_id=1, source_target_pairs={{0,1},{1,2},{2,3},{4,5},{5,6},{6,7},{8,9},{9,10},{10,11},{12,13},{... | collective-permute-start | bytes 823688 | tf_op jit(solution)/shard_map/ppermute | solution.py:14
  27.7 1.3 %collective-permute-start.5 = (f32[2,132,260]{2,1,0:T(8,128)S(1)}, f32[2,132,260]{2,1,0:T(8,128)S(1)}, u32[]{:S(2)}, u32[]{:S(2)}) collective-permute-start(f32[2,132,260]{2,1,0:T(8,128)S(1)} %get-tuple-element.15), channel_id=1, source_target_pairs={{1,0},{2,1},{3,2},{5,4},{6,5},{7,6},{9,8},{10,9},{11,10},{13,12},{... | collective-permute-start | bytes 823688 | tf_op jit(solution)/shard_map/ppermute | solution.py:15
  29.0 4.8 %maximum_maximum_fusion.1 = (f32[16,130,260]{2,1,0:T(8,128)}, f32[16,130,260]{2,1,0:T(8,128)}) fusion(f32[16,128,2]{2,1,0:T(8,128)S(1)} %copy-done.1, f32[16,128,256]{2,1,0:T(8,128)S(1)} %copy-done, f32[16,128,2]{2,1,0:T(8,128)S(1)} %copy.6, f32[16,2,260]{2,1,0:T(2,128)S(1)} %collective-permute-done.2, f32[16,2,260]{2,1,0:T(2,128)S(1)} %collective-permute-done.3), kind=kLoop, calls=%fused_computation.3 | loop fusion | flops 3244800 | bytes 6522880 | tf_op jit(solution)/shard_map/concatenate | solution.py:16
  33.8 1.7 %collective-permute-done.4 = f32[2,132,260]{2,1,0:T(8,128)S(1)} collective-permute-done((f32[2,132,260]{2,1,0:T(8,128)S(1)}, f32[2,132,260]{2,1,0:T(8,128)S(1)}, u32[]{:S(2)}, u32[]{:S(2)}) %collective-permute-start.4) | collective-permute-done | bytes 274592 | tf_op jit(solution)/shard_map/ppermute | solution.py:14
  35.5 10.9 %collective-permute-done.5 = f32[2,132,260]{2,1,0:T(8,128)S(1)} collective-permute-done((f32[2,132,260]{2,1,0:T(8,128)S(1)}, f32[2,132,260]{2,1,0:T(8,128)S(1)}, u32[]{:S(2)}, u32[]{:S(2)}) %collective-permute-start.5) | collective-permute-done | bytes 274592 | tf_op jit(solution)/shard_map/ppermute | solution.py:15
  46.4 6.6 %maximum_maximum_fusion = (f32[18,132,260]{2,1,0:T(8,128)}, f32[18,132,260]{2,1,0:T(8,128)}) fusion(f32[16,2,260]{2,1,0:T(2,128)S(1)} %collective-permute-done.3, f32[16,128,2]{2,1,0:T(8,128)S(1)} %copy-done.1, f32[16,128,256]{2,1,0:T(8,128)S(1)} %copy-done, f32[16,128,2]{2,1,0:T(8,128)S(1)} %copy.6, f32[16,2,260]{2,1,0:T(2,128)S(1)} %collective-permute-done.2, ...), kind=kLoop, calls=%fused_computation.1 | loop fusion | flops 6177600 | bytes 7687680 | tf_op jit(solution)/shard_map/concatenate | solution.py:16
  53.0 20.0 %divide_multiply_fusion.1 = (f32[16,128,256]{2,1,0:T(8,128)}, f32[16,128,256]{2,1,0:T(8,128)}, f32[16,128,256]{2,1,0:T(8,128)}, f32[16,128,256]{2,1,0:T(8,128)}, f32[16,128,256]{2,1,0:T(8,128)}) fusion(f32[16,128,256]{2,1,0:T(8,128)S(1)} %copy-done, f32[18,132,260]{2,1,0:T(8,128)} %get-tuple-element.13, f32[18,132,260]{2,1,0:T(8,128)} %get-tuple-element.12, ...), kind=kLoop, calls=%fused_computation.45 | loop fusion | flops 22020096 | bytes 29392896 | tf_op jit(solution)/shard_map/mul | solution.py:30
  73.0 5.2 %fusion.8 = (f32[16,128,256]{2,1,0:T(8,128)S(1)}, f32[16,128,256]{2,1,0:T(8,128)S(1)}, f32[16,128,256]{2,1,0:T(8,128)S(1)}) fusion(f32[16,128,256]{2,1,0:T(8,128)} %get-tuple-element.8, f32[16,128,256]{2,1,0:T(8,128)S(1)} %copy-done, f32[16,128,256]{2,1,0:T(8,128)} %get-tuple-element.11, f32[16,128,256]{2,1,0:T(8,128)} %get-tuple-element.10, ...), kind=kLoop, calls=%fused_computation.20 | loop fusion | flops 14155776 | bytes 16777216 | tf_op jit(solution)/shard_map/mul | solution.py:31
  78.2 1.2 %copy.16 = f32[2,8,128,256]{3,1,2,0:T(8,128)S(1)} copy(f32[2,8,128,256]{3,2,1,0:T(8,128)S(1)} %bitcast.24) | data formatting | bytes 4194304
  79.4 1.2 %copy.13 = f32[2,8,128,256]{3,1,2,0:T(8,128)S(1)} copy(f32[2,8,128,256]{3,2,1,0:T(8,128)S(1)} %bitcast.23) | data formatting | bytes 4194304
  80.6 0.0 copy-start.2
  80.6 1.2 %copy.15 = f32[2,8,128,256]{3,1,2,0:T(8,128)S(1)} copy(f32[2,8,128,256]{3,2,1,0:T(8,128)S(1)} %bitcast.22) | data formatting | bytes 4194304
  81.9 0.4 copy-done.2
  82.2 1.2 %copy.14 = f32[2,8,128,256]{3,1,2,0:T(8,128)S(1)} copy(f32[2,8,128,256]{3,2,1,0:T(8,128)S(1)} %bitcast.25) | data formatting | bytes 4194304
  83.4 4.5 %multiply_reduce_fusion = (f32[32768]{0:T(1024)S(1)}, f32[32768]{0:T(1024)S(1)}, f32[32768]{0:T(1024)S(1)}, f32[32768]{0:T(1024)S(1)}, f32[16,32768]{1,0:T(8,128)}) fusion(f32[16]{0:T(128)S(1)} %add_multiply_fusion, f32[16,32768]{1,0:T(8,128)S(1)} %bitcast.18, f32[16,32768]{1,0:T(8,128)S(1)} %bitcast.20, f32[16,32768]{1,0:T(8,128)S(1)} %bitcast.21, ...), kind=kOutput, calls=%fused_computation.40 | convolution fusion | flops 107348224 | bytes 11010112 | tf_op jit(solution)/shard_map/dot_general | solution.py:76
  88.1 1.7 %fusion.23 = f32[32768]{0:T(1024)S(1)} fusion(f32[16,32768]{1,0:T(8,128)} %get-tuple-element.27), kind=kLoop, calls=%fused_computation.59 | loop fusion | flops 32768 | bytes 262144 | tf_op jit(solution)/shard_map/exp | solution.py:89
  89.9 10.6 %all_to_all.5 = f32[5,4,32,256]{3,2,0,1:T(8,128)S(1)} all-to-all(f32[5,4,32,256]{3,2,0,1:T(8,128)S(1)} %bitcast_dynamic-update-slice_fusion), channel_id=1, replica_groups=mesh['gx'=2,'gy'=4,'gz'=4] {'gz'}, dimensions={1} | all-to-all | bytes 1310720 | tf_op jit(solution)/shard_map/all_to_all | solution.py:95
  100.6 0.6 slice_bitcast_fusion.2
  101.2 0.6 slice.128
  (15 shorter events, 0.4 us)
Async XLA Ops:
  3.5 8.9 %copy-start = (f32[16,128,256]{2,1,0:T(8,128)S(1)}, f32[16,128,256]{2,1,0:T(8,128)}, u32[]{:S(2)}) copy-start(f32[16,128,256]{2,1,0:T(8,128)} %param.1) | copy-start | bytes 6291460
  5.2 4.0 %collective-permute-start = (f32[16,128,2]{1,0,2:T(8,128)S(1)}, f32[16,128,2]{1,0,2:T(8,128)S(1)}, u32[]{:S(2)}, u32[]{:S(2)}) collective-permute-start(f32[16,128,2]{1,0,2:T(8,128)S(1)} %copy.11), channel_id=1, source_target_pairs={{0,16},{1,17},{2,18},{3,19},{4,20},{5,21},{6,22},{7,23},{8,24},{9,... | collective-permute-start | bytes 49160 | tf_op jit(solution)/shard_map/ppermute | solution.py:14
  7.9 3.1 %collective-permute-start.1 = (f32[16,128,2]{1,0,2:T(8,128)S(1)}, f32[16,128,2]{1,0,2:T(8,128)S(1)}, u32[]{:S(2)}, u32[]{:S(2)}) collective-permute-start(f32[16,128,2]{1,0,2:T(8,128)S(1)} %copy.12), channel_id=1, source_target_pairs={{16,0},{17,1},{18,2},{19,3},{20,4},{21,5},{22,6},{23,7},{24,8},{25... | collective-permute-start | bytes 49160 | tf_op jit(solution)/shard_map/ppermute | solution.py:15
  12.5 11.5 %copy-start.1 = (f32[16,128,2]{2,1,0:T(8,128)S(1)}, f32[16,128,2]{2,1,0:T(8,128)}, u32[]{:S(2)}) copy-start(f32[16,128,2]{2,1,0:T(8,128)} %copy.7) | copy-start | bytes 49156
  13.6 6.1 %collective-permute-start.2 = (f32[16,2,260]{2,1,0:T(2,128)S(1)}, f32[16,2,260]{2,1,0:T(2,128)S(1)}, u32[]{:S(2)}, u32[]{:S(2)}) collective-permute-start(f32[16,2,260]{2,1,0:T(2,128)S(1)} %get-tuple-element.20), channel_id=1, source_target_pairs={{0,4},{4,8},{8,12},{1,5},{5,9},{9,13},{2,6},{6,10},{10,14},{3,7},{... | collective-permute-start | bytes 99848 | tf_op jit(solution)/shard_map/ppermute | solution.py:14
  17.9 6.0 %collective-permute-start.3 = (f32[16,2,260]{2,1,0:T(2,128)S(1)}, f32[16,2,260]{2,1,0:T(2,128)S(1)}, u32[]{:S(2)}, u32[]{:S(2)}) collective-permute-start(f32[16,2,260]{2,1,0:T(2,128)S(1)} %get-tuple-element.21), channel_id=1, source_target_pairs={{4,0},{8,4},{12,8},{5,1},{9,5},{13,9},{6,2},{10,6},{14,10},{7,3},{... | collective-permute-start | bytes 99848 | tf_op jit(solution)/shard_map/ppermute | solution.py:15
  24.3 11.2 %collective-permute-start.4 = (f32[2,132,260]{2,1,0:T(8,128)S(1)}, f32[2,132,260]{2,1,0:T(8,128)S(1)}, u32[]{:S(2)}, u32[]{:S(2)}) collective-permute-start(f32[2,132,260]{2,1,0:T(8,128)S(1)} %get-tuple-element.14), channel_id=1, source_target_pairs={{0,1},{1,2},{2,3},{4,5},{5,6},{6,7},{8,9},{9,10},{10,11},{12,13},{... | collective-permute-start | bytes 823688 | tf_op jit(solution)/shard_map/ppermute | solution.py:14
  27.7 18.7 %collective-permute-start.5 = (f32[2,132,260]{2,1,0:T(8,128)S(1)}, f32[2,132,260]{2,1,0:T(8,128)S(1)}, u32[]{:S(2)}, u32[]{:S(2)}) collective-permute-start(f32[2,132,260]{2,1,0:T(8,128)S(1)} %get-tuple-element.15), channel_id=1, source_target_pairs={{1,0},{2,1},{3,2},{5,4},{6,5},{7,6},{9,8},{10,9},{11,10},{13,12},{... | collective-permute-start | bytes 823688 | tf_op jit(solution)/shard_map/ppermute | solution.py:15
  80.6 1.6 %copy-start.2 = (f32[16,128,256]{2,1,0:T(8,128)S(1)}, f32[16,128,256]{2,1,0:T(8,128)}, u32[]{:S(2)}) copy-start(f32[16,128,256]{2,1,0:T(8,128)} %get-tuple-element.7) | copy-start | bytes 6291460
where the time goes:
time: 102 us
  other arithmetic  39.8 us (39%)
  waiting for transfers between devices  18.6 us (18%)
  starting transfers between devices  14 us (14%)
  local copies, waits for them, and re-layouts  13.5 us (13%)
  blocking collectives  10.6 us (10%)
  matrix products  4.45 us (4%)
    mul x1, other arithmetic, shade(): colour_red = jax.nn.sigmoid(2.0 * sample) * diffuse  20 us
    ppermute x3, waiting for transfers between devices, with_halo(): after = lax.ppermute(initial, axis, down)  16.5 us
    concatenate x2, other arithmetic, with_halo(): shard = jnp.concatenate([before, shard, after], axis=dim)  11.4 us
    all_to_all x1, blocking collectives, on_device(): lax.all_to_all(stacked, 'gz', split_axis=1, concat_axis=1, tiled=True)  10.6 us
    ppermute x3, starting transfers between devices, with_halo(): before = lax.ppermute(last, axis, up)  10.1 us
    unnamed x16, local copies, waits for them, and re-layouts  7.32 us
    mul x1, other arithmetic, shade(): colour_green = jnp.exp(-0.5 * sample * sample) * diffuse  5.18 us
    dot_general x1, matrix products, on_device(): jnp.dot(lower_tri, optical, precision=lax.Precision.HIGHEST, preferred_el...  4.45 us
  transfers between devices with their start and end apart: 6, of which 5 were waited for; matrix products, arithmetic and copies ran while one was open for 5% of the time, Pallas kernels for 0%

commit v1 on v0

--- a/solution.py
+++ b/solution.py
@@ -92,7 +92,10 @@
     piece_rows = cells_y // depth_count
     stacked = partial_value.reshape(5, depth_count, piece_rows, cells_x)
     final_image = blend_depth(
-        lax.all_to_all(stacked, "gz", split_axis=1, concat_axis=1, tiled=True)
+        jnp.concatenate(
+            lax.all_to_all(jnp.stack(jnp.split(stacked, lax.axis_size("gz"), axis=1)), "gz", 0, 0),
+            axis=1,
+        )
     )
     return (final_image[:3], final_image[3], final_image[4])
 

time: 102 us -> 99.7 us (0.977)
  matrix products: 4.45 us -> 3.07 us
  other arithmetic: 39.8 us -> 38.7 us
    dot_general x1, matrix products: 4.45 us -> 3.07 us  [on_device(): jnp.dot(lower_tri, optical, precision=lax.Precision.HIGHEST, preferred_el...]
    exp x1, other arithmetic: 1.65 us -> 0.42 us  [on_device(): jnp.exp(-inclusive[-1])]
  transfers between devices with their start and end apart: 6 -> 6, of which waited for: 5 -> 5; matrix products, arithmetic and copies ran while one was open for 5% -> 6% of each run, Pallas kernels for 0% -> 0%
where the time goes in v1:
time: 99.7 us; the launch traced here: 99.4 us
  other arithmetic  38.7 us (39%)
  waiting for transfers between devices  18.6 us (19%)
  starting transfers between devices  14 us (14%)
  local copies, waits for them, and re-layouts  13.6 us (14%)
  blocking collectives  10.6 us (11%)
  matrix products  3.07 us (3%)
    mul x1, other arithmetic, shade(): colour_red = jax.nn.sigmoid(2.0 * sample) * diffuse  20 us
    ppermute x3, waiting for transfers between devices, with_halo(): after = lax.ppermute(initial, axis, down)  16.5 us
    concatenate x2, other arithmetic, with_halo(): shard = jnp.concatenate([before, shard, after], axis=dim)  11.4 us
    all_to_all x1, blocking collectives, on_device(): lax.all_to_all(jnp.stack(jnp.split(stacked, lax.axis_size('gz'), axis=1))...  10.6 us
    ppermute x3, starting transfers between devices, with_halo(): before = lax.ppermute(last, axis, up)  10.1 us
    unnamed x16, local copies, waits for them, and re-layouts  7.32 us
    mul x1, other arithmetic, shade(): colour_green = jnp.exp(-0.5 * sample * sample) * diffuse  5.18 us
    ppermute x3, starting transfers between devices, with_halo(): after = lax.ppermute(initial, axis, down)  3.88 us
  transfers between devices with their start and end apart: 6, of which 5 were waited for; matrix products, arithmetic and copies ran while one was open for 6% of the time, Pallas kernels for 0%

profile of v1, /device:TPU:0, one launch (start us, length us, event | category | flops | bytes accessed | tf_op | source)
XLA Modules:
  0.0 99.4 jit_solution(3125119165410540349)
XLA Ops:
  0.6 2.9 %fusion.28 = (f32[16,128,2]{2,1,0:T(8,128)}, f32[16,128,2]{2,1,0:T(8,128)S(1)}) fusion(f32[16,128,256]{2,1,0:T(8,128)} %param.1), kind=kLoop, calls=%fused_computation.79 | loop fusion | bytes 65536 | tf_op jit(solution)/shard_map/slice | solution.py:12
  3.5 0.0 copy-start
  3.5 1.7 %copy.18 = f32[16,128,2]{1,0,2:T(8,128)S(1)} copy(f32[16,128,2]{2,1,0:T(8,128)} %get-tuple-element.23) | data formatting | bytes 32768
  5.2 2.4 %collective-permute-start = (f32[16,128,2]{1,0,2:T(8,128)S(1)}, f32[16,128,2]{1,0,2:T(8,128)S(1)}, u32[]{:S(2)}, u32[]{:S(2)}) collective-permute-start(f32[16,128,2]{1,0,2:T(8,128)S(1)} %copy.18), channel_id=1, source_target_pairs={{0,16},{1,17},{2,18},{3,19},{4,20},{5,21},{6,22},{7,23},{8,24},{9,... | collective-permute-start | bytes 49160 | tf_op jit(solution)/shard_map/ppermute | solution.py:14
  7.6 0.3 copy.19
  7.9 1.3 %collective-permute-start.1 = (f32[16,128,2]{1,0,2:T(8,128)S(1)}, f32[16,128,2]{1,0,2:T(8,128)S(1)}, u32[]{:S(2)}, u32[]{:S(2)}) collective-permute-start(f32[16,128,2]{1,0,2:T(8,128)S(1)} %copy.19), channel_id=1, source_target_pairs={{16,0},{17,1},{18,2},{19,3},{20,4},{21,5},{22,6},{23,7},{24,8},{25... | collective-permute-start | bytes 49160 | tf_op jit(solution)/shard_map/ppermute | solution.py:15
  9.2 0.0 collective-permute-done
  9.2 0.4 copy.10
  9.6 1.4 %collective-permute-done.1 = f32[16,128,2]{1,0,2:T(8,128)S(1)} collective-permute-done((f32[16,128,2]{1,0,2:T(8,128)S(1)}, f32[16,128,2]{1,0,2:T(8,128)S(1)}, u32[]{:S(2)}, u32[]{:S(2)}) %collective-permute-start.1) | collective-permute-done | bytes 16416 | tf_op jit(solution)/shard_map/ppermute | solution.py:15
  11.0 1.4 %copy.11 = f32[16,128,2]{2,1,0:T(8,128)} copy(f32[16,128,2]{1,0,2:T(8,128)S(1)} %collective-permute-done.1) | data formatting | bytes 32768 | tf_op jit(solution)/shard_map/ppermute | solution.py:15
  12.5 0.0 copy-done
  12.5 0.0 copy-start.1
  12.5 1.2 %pad_maximum_fusion.12 = (f32[16,2,260]{2,1,0:T(2,128)S(1)}, f32[16,2,260]{2,1,0:T(2,128)S(1)}) fusion(f32[16,128,2]{2,1,0:T(8,128)} %copy.11, f32[16,128,256]{2,1,0:T(8,128)S(1)} %copy-done, f32[16,128,2]{2,1,0:T(8,128)S(1)} %copy.10), kind=kLoop, calls=%fused_computation.69 | loop fusion | flops 33280 | bytes 2196480 | tf_op jit(solution)/shard_map/slice | solution.py:12
  13.6 4.3 %collective-permute-start.2 = (f32[16,2,260]{2,1,0:T(2,128)S(1)}, f32[16,2,260]{2,1,0:T(2,128)S(1)}, u32[]{:S(2)}, u32[]{:S(2)}) collective-permute-start(f32[16,2,260]{2,1,0:T(2,128)S(1)} %get-tuple-element.20), channel_id=1, source_target_pairs={{0,4},{4,8},{8,12},{1,5},{5,9},{9,13},{2,6},{6,10},{10,14},{3,7},{... | collective-permute-start | bytes 99848 | tf_op jit(solution)/shard_map/ppermute | solution.py:14
  17.9 1.3 %collective-permute-start.3 = (f32[16,2,260]{2,1,0:T(2,128)S(1)}, f32[16,2,260]{2,1,0:T(2,128)S(1)}, u32[]{:S(2)}, u32[]{:S(2)}) collective-permute-start(f32[16,2,260]{2,1,0:T(2,128)S(1)} %get-tuple-element.21), channel_id=1, source_target_pairs={{4,0},{8,4},{12,8},{5,1},{9,5},{13,9},{6,2},{10,6},{14,10},{7,3},{... | collective-permute-start | bytes 99848 | tf_op jit(solution)/shard_map/ppermute | solution.py:15
  19.3 0.4 collective-permute-done.2
  19.7 4.3 %collective-permute-done.3 = f32[16,2,260]{2,1,0:T(2,128)S(1)} collective-permute-done((f32[16,2,260]{2,1,0:T(2,128)S(1)}, f32[16,2,260]{2,1,0:T(2,128)S(1)}, u32[]{:S(2)}, u32[]{:S(2)}) %collective-permute-start.3) | collective-permute-done | bytes 33312 | tf_op jit(solution)/shard_map/ppermute | solution.py:15
  23.9 0.0 copy-done.1
  23.9 0.4 pad_maximum_fusion.9
  24.3 3.4 %collective-permute-start.4 = (f32[2,132,260]{2,1,0:T(8,128)S(1)}, f32[2,132,260]{2,1,0:T(8,128)S(1)}, u32[]{:S(2)}, u32[]{:S(2)}) collective-permute-start(f32[2,132,260]{2,1,0:T(8,128)S(1)} %get-tuple-element.14), channel_id=1, source_target_pairs={{0,1},{1,2},{2,3},{4,5},{5,6},{6,7},{8,9},{9,10},{10,11},{12,13},{... | collective-permute-start | bytes 823688 | tf_op jit(solution)/shard_map/ppermute | solution.py:14
  27.7 1.3 %collective-permute-start.5 = (f32[2,132,260]{2,1,0:T(8,128)S(1)}, f32[2,132,260]{2,1,0:T(8,128)S(1)}, u32[]{:S(2)}, u32[]{:S(2)}) collective-permute-start(f32[2,132,260]{2,1,0:T(8,128)S(1)} %get-tuple-element.15), channel_id=1, source_target_pairs={{1,0},{2,1},{3,2},{5,4},{6,5},{7,6},{9,8},{10,9},{11,10},{13,12},{... | collective-permute-start | bytes 823688 | tf_op jit(solution)/shard_map/ppermute | solution.py:15
  29.0 4.8 %maximum_maximum_fusion.1 = (f32[16,130,260]{2,1,0:T(8,128)}, f32[16,130,260]{2,1,0:T(8,128)}) fusion(f32[16,128,2]{2,1,0:T(8,128)S(1)} %copy-done.1, f32[16,128,256]{2,1,0:T(8,128)S(1)} %copy-done, f32[16,128,2]{2,1,0:T(8,128)S(1)} %copy.10, f32[16,2,260]{2,1,0:T(2,128)S(1)} %collective-permute-done.2, f32[16,2,260]{2,1,0:T(2,128)S(1)} %collective-permute-done.3), kind=kLoop, calls=%fused_computation.3 | loop fusion | flops 3244800 | bytes 6522880 | tf_op jit(solution)/shard_map/concatenate | solution.py:16
  33.8 1.7 %collective-permute-done.4 = f32[2,132,260]{2,1,0:T(8,128)S(1)} collective-permute-done((f32[2,132,260]{2,1,0:T(8,128)S(1)}, f32[2,132,260]{2,1,0:T(8,128)S(1)}, u32[]{:S(2)}, u32[]{:S(2)}) %collective-permute-start.4) | collective-permute-done | bytes 274592 | tf_op jit(solution)/shard_map/ppermute | solution.py:14
  35.5 10.9 %collective-permute-done.5 = f32[2,132,260]{2,1,0:T(8,128)S(1)} collective-permute-done((f32[2,132,260]{2,1,0:T(8,128)S(1)}, f32[2,132,260]{2,1,0:T(8,128)S(1)}, u32[]{:S(2)}, u32[]{:S(2)}) %collective-permute-start.5) | collective-permute-done | bytes 274592 | tf_op jit(solution)/shard_map/ppermute | solution.py:15
  46.4 6.6 %maximum_maximum_fusion = (f32[18,132,260]{2,1,0:T(8,128)}, f32[18,132,260]{2,1,0:T(8,128)}) fusion(f32[16,2,260]{2,1,0:T(2,128)S(1)} %collective-permute-done.3, f32[16,128,2]{2,1,0:T(8,128)S(1)} %copy-done.1, f32[16,128,256]{2,1,0:T(8,128)S(1)} %copy-done, f32[16,128,2]{2,1,0:T(8,128)S(1)} %copy.10, f32[16,2,260]{2,1,0:T(2,128)S(1)} %collective-permute-done.2, ...), kind=kLoop, calls=%fused_computation.1 | loop fusion | flops 6177600 | bytes 7687680 | tf_op jit(solution)/shard_map/concatenate | solution.py:16
  53.0 20.0 %divide_multiply_fusion.1 = (f32[16,128,256]{2,1,0:T(8,128)}, f32[16,128,256]{2,1,0:T(8,128)}, f32[16,128,256]{2,1,0:T(8,128)}, f32[16,128,256]{2,1,0:T(8,128)}, f32[16,128,256]{2,1,0:T(8,128)}) fusion(f32[16,128,256]{2,1,0:T(8,128)S(1)} %copy-done, f32[18,132,260]{2,1,0:T(8,128)} %get-tuple-element.13, f32[18,132,260]{2,1,0:T(8,128)} %get-tuple-element.12, ...), kind=kLoop, calls=%fused_computation.45 | loop fusion | flops 22020096 | bytes 29392896 | tf_op jit(solution)/shard_map/mul | solution.py:30
  73.0 5.2 %fusion.8 = (f32[16,128,256]{2,1,0:T(8,128)S(1)}, f32[16,128,256]{2,1,0:T(8,128)S(1)}, f32[16,128,256]{2,1,0:T(8,128)S(1)}) fusion(f32[16,128,256]{2,1,0:T(8,128)} %get-tuple-element.8, f32[16,128,256]{2,1,0:T(8,128)S(1)} %copy-done, f32[16,128,256]{2,1,0:T(8,128)} %get-tuple-element.11, f32[16,128,256]{2,1,0:T(8,128)} %get-tuple-element.10, ...), kind=kLoop, calls=%fused_computation.20 | loop fusion | flops 14155776 | bytes 16777216 | tf_op jit(solution)/shard_map/mul | solution.py:31
  78.2 1.2 %copy.20 = f32[2,8,128,256]{3,1,2,0:T(8,128)S(1)} copy(f32[2,8,128,256]{3,2,1,0:T(8,128)S(1)} %bitcast.45) | data formatting | bytes 4194304
  79.4 1.2 %copy.22 = f32[2,8,128,256]{3,1,2,0:T(8,128)S(1)} copy(f32[2,8,128,256]{3,2,1,0:T(8,128)S(1)} %bitcast.44) | data formatting | bytes 4194304
  80.6 0.0 copy-start.2
  80.6 1.2 %copy.23 = f32[2,8,128,256]{3,1,2,0:T(8,128)S(1)} copy(f32[2,8,128,256]{3,2,1,0:T(8,128)S(1)} %bitcast.43) | data formatting | bytes 4194304
  81.9 0.4 copy-done.2
  82.2 1.2 %copy.21 = f32[2,8,128,256]{3,1,2,0:T(8,128)S(1)} copy(f32[2,8,128,256]{3,2,1,0:T(8,128)S(1)} %bitcast.46) | data formatting | bytes 4194304
  83.4 3.1 %multiply_reduce_fusion = (f32[32768]{0:T(1024)S(1)}, f32[32768]{0:T(1024)S(1)}, f32[32768]{0:T(1024)S(1)}, f32[32768]{0:T(1024)S(1)}, f32[16,32768]{1,0:T(8,128)S(1)}) fusion(f32[16]{0:T(128)S(1)} %add_multiply_fusion, f32[16,32768]{1,0:T(8,128)S(1)} %bitcast.41, f32[16,32768]{1,0:T(8,128)S(1)} %bitcast.40, f32[16,32768]{1,0:T(8,128)S(1)} %bitcast.42, ...), kind=kOutput, calls=%fused_computation.40 | convolution fusion | flops 107348224 | bytes 11010112 | tf_op jit(solution)/shard_map/dot_general | solution.py:76
  86.7 0.4 fusion.24
  87.3 0.1 pad_maximum_fusion.4
  87.4 10.6 %all_to_all.5 = f32[4,5,1,32,256]{4,3,2,1,0:T(8,128)S(1)} all-to-all(f32[4,5,1,32,256]{4,3,2,1,0:T(8,128)S(1)} %pad_maximum_fusion.4), channel_id=1, replica_groups=mesh['gx'=2,'gy'=4,'gz'=4] {'gz'}, dimensions={0} | all-to-all | bytes 1310720 | tf_op jit(solution)/shard_map/all_to_all | solution.py:96
  98.1 0.6 slice_bitcast_fusion.7
  98.8 0.6 slice.133
  (16 shorter events, 0.4 us)
Async XLA Ops:
  3.5 8.9 %copy-start = (f32[16,128,256]{2,1,0:T(8,128)S(1)}, f32[16,128,256]{2,1,0:T(8,128)}, u32[]{:S(2)}) copy-start(f32[16,128,256]{2,1,0:T(8,128)} %param.1) | copy-start | bytes 6291460
  5.2 4.0 %collective-permute-start = (f32[16,128,2]{1,0,2:T(8,128)S(1)}, f32[16,128,2]{1,0,2:T(8,128)S(1)}, u32[]{:S(2)}, u32[]{:S(2)}) collective-permute-start(f32[16,128,2]{1,0,2:T(8,128)S(1)} %copy.18), channel_id=1, source_target_pairs={{0,16},{1,17},{2,18},{3,19},{4,20},{5,21},{6,22},{7,23},{8,24},{9,... | collective-permute-start | bytes 49160 | tf_op jit(solution)/shard_map/ppermute | solution.py:14
  7.9 3.1 %collective-permute-start.1 = (f32[16,128,2]{1,0,2:T(8,128)S(1)}, f32[16,128,2]{1,0,2:T(8,128)S(1)}, u32[]{:S(2)}, u32[]{:S(2)}) collective-permute-start(f32[16,128,2]{1,0,2:T(8,128)S(1)} %copy.19), channel_id=1, source_target_pairs={{16,0},{17,1},{18,2},{19,3},{20,4},{21,5},{22,6},{23,7},{24,8},{25... | collective-permute-start | bytes 49160 | tf_op jit(solution)/shard_map/ppermute | solution.py:15
  12.5 11.5 %copy-start.1 = (f32[16,128,2]{2,1,0:T(8,128)S(1)}, f32[16,128,2]{2,1,0:T(8,128)}, u32[]{:S(2)}) copy-start(f32[16,128,2]{2,1,0:T(8,128)} %copy.11) | copy-start | bytes 49156
  13.6 6.1 %collective-permute-start.2 = (f32[16,2,260]{2,1,0:T(2,128)S(1)}, f32[16,2,260]{2,1,0:T(2,128)S(1)}, u32[]{:S(2)}, u32[]{:S(2)}) collective-permute-start(f32[16,2,260]{2,1,0:T(2,128)S(1)} %get-tuple-element.20), channel_id=1, source_target_pairs={{0,4},{4,8},{8,12},{1,5},{5,9},{9,13},{2,6},{6,10},{10,14},{3,7},{... | collective-permute-start | bytes 99848 | tf_op jit(solution)/shard_map/ppermute | solution.py:14
  17.9 6.0 %collective-permute-start.3 = (f32[16,2,260]{2,1,0:T(2,128)S(1)}, f32[16,2,260]{2,1,0:T(2,128)S(1)}, u32[]{:S(2)}, u32[]{:S(2)}) collective-permute-start(f32[16,2,260]{2,1,0:T(2,128)S(1)} %get-tuple-element.21), channel_id=1, source_target_pairs={{4,0},{8,4},{12,8},{5,1},{9,5},{13,9},{6,2},{10,6},{14,10},{7,3},{... | collective-permute-start | bytes 99848 | tf_op jit(solution)/shard_map/ppermute | solution.py:15
  24.3 11.2 %collective-permute-start.4 = (f32[2,132,260]{2,1,0:T(8,128)S(1)}, f32[2,132,260]{2,1,0:T(8,128)S(1)}, u32[]{:S(2)}, u32[]{:S(2)}) collective-permute-start(f32[2,132,260]{2,1,0:T(8,128)S(1)} %get-tuple-element.14), channel_id=1, source_target_pairs={{0,1},{1,2},{2,3},{4,5},{5,6},{6,7},{8,9},{9,10},{10,11},{12,13},{... | collective-permute-start | bytes 823688 | tf_op jit(solution)/shard_map/ppermute | solution.py:14
  27.7 18.7 %collective-permute-start.5 = (f32[2,132,260]{2,1,0:T(8,128)S(1)}, f32[2,132,260]{2,1,0:T(8,128)S(1)}, u32[]{:S(2)}, u32[]{:S(2)}) collective-permute-start(f32[2,132,260]{2,1,0:T(8,128)S(1)} %get-tuple-element.15), channel_id=1, source_target_pairs={{1,0},{2,1},{3,2},{5,4},{6,5},{7,6},{9,8},{10,9},{11,10},{13,12},{... | collective-permute-start | bytes 823688 | tf_op jit(solution)/shard_map/ppermute | solution.py:15
  80.6 1.6 %copy-start.2 = (f32[16,128,256]{2,1,0:T(8,128)S(1)}, f32[16,128,256]{2,1,0:T(8,128)}, u32[]{:S(2)}) copy-start(f32[16,128,256]{2,1,0:T(8,128)} %get-tuple-element.7) | copy-start | bytes 6291460
